TPU v7x, 32 devices: a whole 2x2x4 slice. The times are simulated.
32 devices in a mesh: section: 4 (over z), dom: 8 (over y, x, core).
Axes of the slice: x: 2, y: 2, z: 4, core: 2. Of those that a mesh axis runs over, the one named last changes fastest.
Arguments:
- top_grad: bfloat16 [1, 4096, 512], P(None, 'dom'), may hold values from -6 to 6
- agg_in: bfloat16 [4, 1, 4096, 512], P('section', None, 'dom'), may hold values from -6 to 6
- pre_act: bfloat16 [4, 1, 4096, 512], P('section', None, 'dom'), may hold values from -6 to 6
- weights: bfloat16 [4, 512, 512], P('section'), may hold values from -0.25 to 0.25
- local_adj_t: bfloat16 [1, 4096, 512], P(None, 'dom'), may hold values from -0.25 to 0.25
- tiles: bfloat16 [1, 24, 128, 128], P(None, 'dom'), may hold values from -0.625 to 0.625
- tile_source: int32 [1, 24], P(None, 'dom'), may hold values from 0 to 3
- owner_rows: int32 [1, 8, 8, 48], P(None, 'dom'), may hold values from 0 to 511, as said below
- counts: int32 [1, 8, 8], P(None, 'dom'), may hold values from 1 to 48, as said below
Outputs:
- layer_grads: bfloat16 [4, 1, 4096, 512], P('section', None, 'dom')
- weight_grads: float32 [4, 512, 512], P('section', 'dom')
Inputs may be any that keep to these rules, and one draw needn't show every extreme that they name: `owner_rows`: distinct local nodes of the owner for the slots of one source; only the first counts slots are live. `counts`: in every group one owner part receives all 48 slots from every source part.
All inputs are finite; a program needn't handle non-finite values.
Results may differ from a plain program's by a relative error of at most 0.022.
Values may be sent and summed in bfloat16 or wider, within the bound.
A program may use at most 64 MiB of HBM per device.

v0:
```python
import math

import jax
import jax.numpy as jnp
from jax import lax
from jax.sharding import PartitionSpec as P


def from_behind(block, axis, distance):
    devices = range(lax.axis_size(axis))
    route = [(i - distance, i) for i in devices if i - distance in devices]
    return lax.ppermute(block, axis, route)


def per_device(
    top_grad, agg_in, pre_act, weights, local_adj_t, tiles, tile_source, owner_rows, counts
):
    sections = lax.axis_size("section")
    part_count = lax.axis_size("dom")
    section_pos = lax.axis_index("section")
    group_count, row_count, feat_width = top_grad.shape
    tile_size = tiles.shape[2]
    slot_count = owner_rows.shape[3]
    weight = weights[0]
    agg_all = agg_in[0]
    pre_all = pre_act[0]
    tick_count = group_count + sections - 1
    scale_factor = 1.0 / math.sqrt(group_count * row_count * part_count)
    slot_index = jnp.arange(slot_count)

    def make_mirror(grad_y, group_pick):
        block_pick = lax.dynamic_index_in_dim(tile_source, group_pick, 0, keepdims=False)
        blocks = grad_y.reshape(row_count // tile_size, tile_size, feat_width)[block_pick]
        tile_set = lax.dynamic_index_in_dim(tiles, group_pick, 0, keepdims=False)
        partial_value = jnp.einsum(
            "brt,btf->brf", tile_set, blocks, preferred_element_type=jnp.float32
        )
        return partial_value.reshape(part_count, slot_count, feat_width).astype(jnp.bfloat16)

    def slot_targets(group_pick):
        targets = lax.dynamic_index_in_dim(owner_rows, group_pick, 0, keepdims=False)[0]
        live_count = lax.dynamic_index_in_dim(counts, group_pick, 0, keepdims=False)[0]
        is_valid = slot_index[None, :] < live_count[:, None]
        return jnp.where(is_valid, targets, row_count).reshape(-1)

    def boundary_sum(grad_y, group_pick):
        mirror = make_mirror(grad_y, group_pick)
        target_index = slot_targets(group_pick)
        received = lax.all_to_all(mirror, "dom", split_axis=0, concat_axis=0, tiled=True)
        flat = received.reshape(-1, feat_width).astype(jnp.float32)
        return (
            jnp.zeros((row_count, feat_width), jnp.float32).at[target_index].add(flat, mode="drop")
        )

    def run_tick(tick_step, state_tuple):
        incoming, grads_out, weight_acc = state_tuple
        group_now = tick_step - (sections - 1 - section_pos)
        active = (group_now >= 0) & (group_now < group_count)
        group_pick = jnp.clip(group_now, 0, group_count - 1)
        top_block = lax.dynamic_index_in_dim(top_grad, group_pick, 0, keepdims=False)
        gradient = jnp.where(section_pos == sections - 1, top_block, incoming)
        pre_block = lax.dynamic_index_in_dim(pre_all, group_pick, 0, keepdims=False)
        agg_block = lax.dynamic_index_in_dim(agg_all, group_pick, 0, keepdims=False)
        adj_block = lax.dynamic_index_in_dim(local_adj_t, group_pick, 0, keepdims=False)
        masked = jnp.where(pre_block > 0, gradient, jnp.zeros_like(gradient))
        grad_y = jnp.einsum("ib,ab->ia", masked, weight, preferred_element_type=jnp.float32).astype(
            jnp.bfloat16
        )
        boundary = boundary_sum(grad_y, group_pick)
        dw_term = jnp.einsum("ia,ib->ab", agg_block, masked, preferred_element_type=jnp.float32)
        local_sum = jnp.dot(adj_block, grad_y, preferred_element_type=jnp.float32)
        total_grad = (local_sum + boundary).astype(jnp.bfloat16)
        weight_acc = weight_acc + jnp.where(active, dw_term, jnp.zeros_like(dw_term))
        updated = lax.dynamic_update_index_in_dim(grads_out, total_grad, group_pick, 0)
        grads_out = jnp.where(active, updated, grads_out)
        passed = from_behind(total_grad, "section", -1)
        return (passed, grads_out, weight_acc)

    start_state = (
        jnp.zeros((row_count, feat_width), jnp.bfloat16),
        jnp.zeros((group_count, row_count, feat_width), jnp.bfloat16),
        jnp.zeros((feat_width, feat_width), jnp.float32),
    )
    final_state = lax.fori_loop(0, tick_count, run_tick, start_state)
    grads_out = final_state[1]
    summed = lax.psum_scatter(final_state[2], "dom", scatter_dimension=0, tiled=True)
    return (grads_out[None], (summed * scale_factor)[None])


def solution(mesh):
    in_specs = (
        P(None, "dom", None),
        P("section", None, "dom", None),
        P("section", None, "dom", None),
        P("section", None, None),
        P(None, "dom", None),
        P(None, "dom", None, None),
        P(None, "dom"),
        P(None, "dom", None, None),
        P(None, "dom", None),
    )
    out_specs = (P("section", None, "dom", None), P("section", "dom", None))
    return jax.shard_map(
        per_device, mesh=mesh, in_specs=in_specs, out_specs=out_specs, check_vma=False
    )
```

profile of v0, /device:TPU:0, one launch (start us, length us, event | category | flops | bytes accessed | tf_op | source)
XLA Modules:
  0.0 198.1 jit_solution(14050655030064520697)
XLA Ops:
  8.8 142.4 %while.21 = (s32[]{:T(128)}, bf16[512,512]{1,0:T(8,128)(2,1)S(1)}, bf16[1,512,512]{2,1,0:T(8,128)(2,1)}, f32[512,512]{0,1:T(8,128)}, bf16[1,512,512]{2,1,0:T(8,1...) while((s32[]{:T(128)}, bf16[512,512]{1,0:T(8,128)(2,1)S(1)}, ...), condition=%wide.wide.region_2.3_spmd.clone, body=%wide.wide.region_0.2_spmd.clone.sunk | while | flops 858852224 | bytes 35103768 | solution.py:84
  8.8 1.2 bitcast_select_fusion.7
  12.4 5.3 %all-to-all-start = ((bf16[8,48,512]{2,1,0:T(8,128)(2,1)}), bf16[8,48,512]{2,1,0:T(8,128)(2,1)S(1)}, u32[]{:S(2)}, u32[]{:S(2)}) async-start(bf16[8,48,512]{2,1,0:T(8,128)(2,1)} %bitcast.102), calls=%async_computation | async-start | bytes 786432 | tf_op jit(solution)/shard_map/while/body/eval_jaxpr/all_to_all | solution.py:49
  18.7 7.3 %all-to-all-done = bf16[8,48,512]{2,1,0:T(8,128)(2,1)S(1)} async-done(((bf16[8,48,512]{2,1,0:T(8,128)(2,1)}), bf16[8,48,512]{2,1,0:T(8,128)(2,1)S(1)}, u32[]{:S(2)}, u32[]{:S(2)}) %all-to-all-start) | async-done | bytes 393248 | tf_op jit(solution)/shard_map/while/body/eval_jaxpr/all_to_all | solution.py:49
  26.0 3.3 %scatter_custom_fusion.8 = f32[512,512]{1,0:T(8,128)S(1)} fusion(f32[512,512]{1,0:T(8,128)S(1)} %copy.15, s32[384]{0:T(512)S(1)} %fusion.49, bf16[384,512]{1,0:T(8,128)(2,1)S(1)} %bitcast.105), kind=kCustom, calls=%fused_computation.10.clone.clone.1 | custom fusion | flops 393216 | bytes 1441792 | tf_op jit(solution)/shard_map/while/body/eval_jaxpr/scatter-add | solution.py:52
  30.4 1.3 collective-permute-start
  31.7 1.6 fusion.51
  33.3 11.5 %collective-permute-done = bf16[512,512]{1,0:T(8,128)(2,1)S(1)} collective-permute-done((bf16[512,512]{1,0:T(8,128)(2,1)}, bf16[512,512]{1,0:T(8,128)(2,1)S(1)}, u32[]{:S(2)}, u32[]{:S(2)}) %collective-permute-start) | collective-permute-done | bytes 524320 | tf_op jit(solution)/shard_map/while/body/eval_jaxpr/ppermute | solution.py:12
  48.5 3.6 %all-to-all-start = ((bf16[8,48,512]{2,1,0:T(8,128)(2,1)}), bf16[8,48,512]{2,1,0:T(8,128)(2,1)S(1)}, u32[]{:S(2)}, u32[]{:S(2)}) async-start(bf16[8,48,512]{2,1,0:T(8,128)(2,1)} %bitcast.102), calls=%async_computation | async-start | bytes 786432 | tf_op jit(solution)/shard_map/while/body/eval_jaxpr/all_to_all | solution.py:49
  53.1 7.2 %all-to-all-done = bf16[8,48,512]{2,1,0:T(8,128)(2,1)S(1)} async-done(((bf16[8,48,512]{2,1,0:T(8,128)(2,1)}), bf16[8,48,512]{2,1,0:T(8,128)(2,1)S(1)}, u32[]{:S(2)}, u32[]{:S(2)}) %all-to-all-start) | async-done | bytes 393248 | tf_op jit(solution)/shard_map/while/body/eval_jaxpr/all_to_all | solution.py:49
  60.3 3.3 %scatter_custom_fusion.8 = f32[512,512]{1,0:T(8,128)S(1)} fusion(f32[512,512]{1,0:T(8,128)S(1)} %copy.15, s32[384]{0:T(512)S(1)} %fusion.49, bf16[384,512]{1,0:T(8,128)(2,1)S(1)} %bitcast.105), kind=kCustom, calls=%fused_computation.10.clone.clone.1 | custom fusion | flops 393216 | bytes 1441792 | tf_op jit(solution)/shard_map/while/body/eval_jaxpr/scatter-add | solution.py:52
  63.6 2.2 %bitcast_select_fusion.8 = (bf16[1,512,512]{2,1,0:T(8,128)(2,1)}, bf16[512,512]{1,0:T(8,128)(2,1)}) fusion(bf16[1,512,512]{2,1,0:T(8,128)(2,1)} %get-tuple-element.613, pred[]{:T(512)S(6)} %compare.4, pred[]{:T(512)S(6)} %and.13, f32[512,512]{1,0:T(8,128)S(1)} %scatter_custom_fusion.8), kind=kLoop, calls=%fused_computation.13.clone.clone.1 | loop fusion | flops 786432 | bytes 2621442 | tf_op jit(solution)/shard_map/while/body/eval_jaxpr/jit(_where)/select_n | solution.py:75
  65.8 1.3 collective-permute-start
  67.1 1.6 fusion.51
  68.7 11.5 %collective-permute-done = bf16[512,512]{1,0:T(8,128)(2,1)S(1)} collective-permute-done((bf16[512,512]{1,0:T(8,128)(2,1)}, bf16[512,512]{1,0:T(8,128)(2,1)S(1)}, u32[]{:S(2)}, u32[]{:S(2)}) %collective-permute-start) | collective-permute-done | bytes 524320 | tf_op jit(solution)/shard_map/while/body/eval_jaxpr/ppermute | solution.py:12
  83.9 3.6 %all-to-all-start = ((bf16[8,48,512]{2,1,0:T(8,128)(2,1)}), bf16[8,48,512]{2,1,0:T(8,128)(2,1)S(1)}, u32[]{:S(2)}, u32[]{:S(2)}) async-start(bf16[8,48,512]{2,1,0:T(8,128)(2,1)} %bitcast.102), calls=%async_computation | async-start | bytes 786432 | tf_op jit(solution)/shard_map/while/body/eval_jaxpr/all_to_all | solution.py:49
  88.5 7.2 %all-to-all-done = bf16[8,48,512]{2,1,0:T(8,128)(2,1)S(1)} async-done(((bf16[8,48,512]{2,1,0:T(8,128)(2,1)}), bf16[8,48,512]{2,1,0:T(8,128)(2,1)S(1)}, u32[]{:S(2)}, u32[]{:S(2)}) %all-to-all-start) | async-done | bytes 393248 | tf_op jit(solution)/shard_map/while/body/eval_jaxpr/all_to_all | solution.py:49
  95.7 3.3 %scatter_custom_fusion.8 = f32[512,512]{1,0:T(8,128)S(1)} fusion(f32[512,512]{1,0:T(8,128)S(1)} %copy.15, s32[384]{0:T(512)S(1)} %fusion.49, bf16[384,512]{1,0:T(8,128)(2,1)S(1)} %bitcast.105), kind=kCustom, calls=%fused_computation.10.clone.clone.1 | custom fusion | flops 393216 | bytes 1441792 | tf_op jit(solution)/shard_map/while/body/eval_jaxpr/scatter-add | solution.py:52
  99.0 2.2 %bitcast_select_fusion.8 = (bf16[1,512,512]{2,1,0:T(8,128)(2,1)}, bf16[512,512]{1,0:T(8,128)(2,1)}) fusion(bf16[1,512,512]{2,1,0:T(8,128)(2,1)} %get-tuple-element.613, pred[]{:T(512)S(6)} %compare.4, pred[]{:T(512)S(6)} %and.13, f32[512,512]{1,0:T(8,128)S(1)} %scatter_custom_fusion.8), kind=kLoop, calls=%fused_computation.13.clone.clone.1 | loop fusion | flops 786432 | bytes 2621442 | tf_op jit(solution)/shard_map/while/body/eval_jaxpr/jit(_where)/select_n | solution.py:75
  101.2 1.3 collective-permute-start
  102.5 1.6 fusion.51
  104.2 11.5 %collective-permute-done = bf16[512,512]{1,0:T(8,128)(2,1)S(1)} collective-permute-done((bf16[512,512]{1,0:T(8,128)(2,1)}, bf16[512,512]{1,0:T(8,128)(2,1)S(1)}, u32[]{:S(2)}, u32[]{:S(2)}) %collective-permute-start) | collective-permute-done | bytes 524320 | tf_op jit(solution)/shard_map/while/body/eval_jaxpr/ppermute | solution.py:12
  119.3 3.6 %all-to-all-start = ((bf16[8,48,512]{2,1,0:T(8,128)(2,1)}), bf16[8,48,512]{2,1,0:T(8,128)(2,1)S(1)}, u32[]{:S(2)}, u32[]{:S(2)}) async-start(bf16[8,48,512]{2,1,0:T(8,128)(2,1)} %bitcast.102), calls=%async_computation | async-start | bytes 786432 | tf_op jit(solution)/shard_map/while/body/eval_jaxpr/all_to_all | solution.py:49
  124.0 7.2 %all-to-all-done = bf16[8,48,512]{2,1,0:T(8,128)(2,1)S(1)} async-done(((bf16[8,48,512]{2,1,0:T(8,128)(2,1)}), bf16[8,48,512]{2,1,0:T(8,128)(2,1)S(1)}, u32[]{:S(2)}, u32[]{:S(2)}) %all-to-all-start) | async-done | bytes 393248 | tf_op jit(solution)/shard_map/while/body/eval_jaxpr/all_to_all | solution.py:49
  131.1 3.3 %scatter_custom_fusion.8 = f32[512,512]{1,0:T(8,128)S(1)} fusion(f32[512,512]{1,0:T(8,128)S(1)} %copy.15, s32[384]{0:T(512)S(1)} %fusion.49, bf16[384,512]{1,0:T(8,128)(2,1)S(1)} %bitcast.105), kind=kCustom, calls=%fused_computation.10.clone.clone.1 | custom fusion | flops 393216 | bytes 1441792 | tf_op jit(solution)/shard_map/while/body/eval_jaxpr/scatter-add | solution.py:52
  134.4 2.2 %bitcast_select_fusion.8 = (bf16[1,512,512]{2,1,0:T(8,128)(2,1)}, bf16[512,512]{1,0:T(8,128)(2,1)}) fusion(bf16[1,512,512]{2,1,0:T(8,128)(2,1)} %get-tuple-element.613, pred[]{:T(512)S(6)} %compare.4, pred[]{:T(512)S(6)} %and.13, f32[512,512]{1,0:T(8,128)S(1)} %scatter_custom_fusion.8), kind=kLoop, calls=%fused_computation.13.clone.clone.1 | loop fusion | flops 786432 | bytes 2621442 | tf_op jit(solution)/shard_map/while/body/eval_jaxpr/jit(_where)/select_n | solution.py:75
  136.6 1.3 collective-permute-start
  137.9 1.6 fusion.51
  139.6 11.5 %collective-permute-done = bf16[512,512]{1,0:T(8,128)(2,1)S(1)} collective-permute-done((bf16[512,512]{1,0:T(8,128)(2,1)}, bf16[512,512]{1,0:T(8,128)(2,1)S(1)}, u32[]{:S(2)}, u32[]{:S(2)}) %collective-permute-start) | collective-permute-done | bytes 524320 | tf_op jit(solution)/shard_map/while/body/eval_jaxpr/ppermute | solution.py:12
  151.1 2.5 %copy.12 = f32[512,512]{1,0:T(8,128)} copy(f32[512,512]{0,1:T(8,128)} %get-tuple-element.653) | data formatting | bytes 2097152 | tf_op jit(solution)/shard_map/while | solution.py:84
  153.7 35.9 %reduce-scatter.2.cloned.1.call-done = f32[64,512]{1,0:T(8,128)} async-done(((f32[512,512]{1,0:T(8,128)}), f32[64,512]{1,0:T(8,128)}) %reduce-scatter.2.cloned.1.call-update) | async-done | bytes 131088 | tf_op jit(solution)/shard_map/reduce_scatter | solution.py:86
  189.6 1.6 multiply_bitcast_fusion
  (104 shorter events, 19.7 us)
Async XLA Ops:
  7.2 1.1 copy-start.2
  7.2 182.5 %reduce-scatter.2.cloned.1.call-start = ((), (), s32[]{:S(2)}) async-start(), calls=%async_computation.2 | async-start | bytes 1179648 | tf_op jit(solution)/shard_map/reduce_scatter | solution.py:86
  8.8 1.2 copy-start.4
  10.5 0.9 copy-start.6
  12.4 5.5 %copy-start.5 = (bf16[1,512,512]{2,1,0:T(8,128)(2,1)S(1)}, bf16[1,512,512]{2,1,0:T(8,128)(2,1)}, u32[]{:S(2)}) copy-start(bf16[1,512,512]{2,1,0:T(8,128)(2,1)} %get-tuple-element.637) | copy-start | bytes 1572868 | tf_op jit(solution)/shard_map/while
  12.4 13.6 %all-to-all-start = ((bf16[8,48,512]{2,1,0:T(8,128)(2,1)}), bf16[8,48,512]{2,1,0:T(8,128)(2,1)S(1)}, u32[]{:S(2)}, u32[]{:S(2)}) async-start(bf16[8,48,512]{2,1,0:T(8,128)(2,1)} %bitcast.102), calls=%async_computation | async-start | bytes 786432 | tf_op jit(solution)/shard_map/while/body/eval_jaxpr/all_to_all | solution.py:49
  29.3 2.4 %copy-start = (f32[512,512]{0,1:T(8,128)S(1)}, f32[512,512]{0,1:T(8,128)}, u32[]{:S(2)}) copy-start(f32[512,512]{0,1:T(8,128)} %get-tuple-element.614) | copy-start | bytes 3145732 | tf_op jit(solution)/shard_map/while
  30.4 14.5 %collective-permute-start = (bf16[512,512]{1,0:T(8,128)(2,1)}, bf16[512,512]{1,0:T(8,128)(2,1)S(1)}, u32[]{:S(2)}, u32[]{:S(2)}) collective-permute-start(bf16[512,512]{1,0:T(8,128)(2,1)} %get-tuple-element.591), channel_id=1, source_target_pairs={{8,0},{16,8},{24,16},{9,1},{17,9},{25,17},{10,2},{18,10},{26,18},{... | collective-permute-start | bytes 1572872 | tf_op jit(solution)/shard_map/while/body/eval_jaxpr/ppermute | solution.py:12
  31.7 13.2 %copy-start.3 = (bf16[1,1,512,512]{3,2,1,0:T(8,128)(2,1)S(1)}, bf16[1,1,512,512]{3,2,1,0:T(8,128)(2,1)}, u32[]{:S(2)}) copy-start(bf16[1,1,512,512]{3,2,1,0:T(8,128)(2,1)} %get-tuple-element.668) | copy-start | bytes 1572868 | tf_op jit(solution)/shard_map/while
  33.3 11.6 %copy-start.1 = (f32[512,512]{0,1:T(8,128)}, f32[512,512]{0,1:T(8,128)S(1)}, u32[]{:S(2)}) copy-start(f32[512,512]{0,1:T(8,128)S(1)} %fusion.51) | copy-start | bytes 3145732 | tf_op jit(solution)/shard_map/while
  44.9 1.2 copy-start.4
  46.6 0.9 copy-start.6
  48.5 3.8 %copy-start.5 = (bf16[1,512,512]{2,1,0:T(8,128)(2,1)S(1)}, bf16[1,512,512]{2,1,0:T(8,128)(2,1)}, u32[]{:S(2)}) copy-start(bf16[1,512,512]{2,1,0:T(8,128)(2,1)} %get-tuple-element.637) | copy-start | bytes 1572868 | tf_op jit(solution)/shard_map/while
  48.5 11.8 %all-to-all-start = ((bf16[8,48,512]{2,1,0:T(8,128)(2,1)}), bf16[8,48,512]{2,1,0:T(8,128)(2,1)S(1)}, u32[]{:S(2)}, u32[]{:S(2)}) async-start(bf16[8,48,512]{2,1,0:T(8,128)(2,1)} %bitcast.102), calls=%async_computation | async-start | bytes 786432 | tf_op jit(solution)/shard_map/while/body/eval_jaxpr/all_to_all | solution.py:49
  63.6 3.5 %copy-start = (f32[512,512]{0,1:T(8,128)S(1)}, f32[512,512]{0,1:T(8,128)}, u32[]{:S(2)}) copy-start(f32[512,512]{0,1:T(8,128)} %get-tuple-element.614) | copy-start | bytes 3145732 | tf_op jit(solution)/shard_map/while
  65.8 14.5 %collective-permute-start = (bf16[512,512]{1,0:T(8,128)(2,1)}, bf16[512,512]{1,0:T(8,128)(2,1)S(1)}, u32[]{:S(2)}, u32[]{:S(2)}) collective-permute-start(bf16[512,512]{1,0:T(8,128)(2,1)} %get-tuple-element.591), channel_id=1, source_target_pairs={{8,0},{16,8},{24,16},{9,1},{17,9},{25,17},{10,2},{18,10},{26,18},{... | collective-permute-start | bytes 1572872 | tf_op jit(solution)/shard_map/while/body/eval_jaxpr/ppermute | solution.py:12
  67.1 13.2 %copy-start.3 = (bf16[1,1,512,512]{3,2,1,0:T(8,128)(2,1)S(1)}, bf16[1,1,512,512]{3,2,1,0:T(8,128)(2,1)}, u32[]{:S(2)}) copy-start(bf16[1,1,512,512]{3,2,1,0:T(8,128)(2,1)} %get-tuple-element.668) | copy-start | bytes 1572868 | tf_op jit(solution)/shard_map/while
  68.7 11.6 %copy-start.1 = (f32[512,512]{0,1:T(8,128)}, f32[512,512]{0,1:T(8,128)S(1)}, u32[]{:S(2)}) copy-start(f32[512,512]{0,1:T(8,128)S(1)} %fusion.51) | copy-start | bytes 3145732 | tf_op jit(solution)/shard_map/while
  80.3 1.2 copy-start.4
  83.9 3.8 %copy-start.5 = (bf16[1,512,512]{2,1,0:T(8,128)(2,1)S(1)}, bf16[1,512,512]{2,1,0:T(8,128)(2,1)}, u32[]{:S(2)}) copy-start(bf16[1,512,512]{2,1,0:T(8,128)(2,1)} %get-tuple-element.637) | copy-start | bytes 1572868 | tf_op jit(solution)/shard_map/while
  83.9 11.8 %all-to-all-start = ((bf16[8,48,512]{2,1,0:T(8,128)(2,1)}), bf16[8,48,512]{2,1,0:T(8,128)(2,1)S(1)}, u32[]{:S(2)}, u32[]{:S(2)}) async-start(bf16[8,48,512]{2,1,0:T(8,128)(2,1)} %bitcast.102), calls=%async_computation | async-start | bytes 786432 | tf_op jit(solution)/shard_map/while/body/eval_jaxpr/all_to_all | solution.py:49
  99.0 3.5 %copy-start = (f32[512,512]{0,1:T(8,128)S(1)}, f32[512,512]{0,1:T(8,128)}, u32[]{:S(2)}) copy-start(f32[512,512]{0,1:T(8,128)} %get-tuple-element.614) | copy-start | bytes 3145732 | tf_op jit(solution)/shard_map/while
  101.2 14.5 %collective-permute-start = (bf16[512,512]{1,0:T(8,128)(2,1)}, bf16[512,512]{1,0:T(8,128)(2,1)S(1)}, u32[]{:S(2)}, u32[]{:S(2)}) collective-permute-start(bf16[512,512]{1,0:T(8,128)(2,1)} %get-tuple-element.591), channel_id=1, source_target_pairs={{8,0},{16,8},{24,16},{9,1},{17,9},{25,17},{10,2},{18,10},{26,18},{... | collective-permute-start | bytes 1572872 | tf_op jit(solution)/shard_map/while/body/eval_jaxpr/ppermute | solution.py:12
  102.5 13.2 %copy-start.3 = (bf16[1,1,512,512]{3,2,1,0:T(8,128)(2,1)S(1)}, bf16[1,1,512,512]{3,2,1,0:T(8,128)(2,1)}, u32[]{:S(2)}) copy-start(bf16[1,1,512,512]{3,2,1,0:T(8,128)(2,1)} %get-tuple-element.668) | copy-start | bytes 1572868 | tf_op jit(solution)/shard_map/while
  104.2 11.6 %copy-start.1 = (f32[512,512]{0,1:T(8,128)}, f32[512,512]{0,1:T(8,128)S(1)}, u32[]{:S(2)}) copy-start(f32[512,512]{0,1:T(8,128)S(1)} %fusion.51) | copy-start | bytes 3145732 | tf_op jit(solution)/shard_map/while
  115.7 1.2 copy-start.4
  119.3 3.8 %copy-start.5 = (bf16[1,512,512]{2,1,0:T(8,128)(2,1)S(1)}, bf16[1,512,512]{2,1,0:T(8,128)(2,1)}, u32[]{:S(2)}) copy-start(bf16[1,512,512]{2,1,0:T(8,128)(2,1)} %get-tuple-element.637) | copy-start | bytes 1572868 | tf_op jit(solution)/shard_map/while
  119.3 11.8 %all-to-all-start = ((bf16[8,48,512]{2,1,0:T(8,128)(2,1)}), bf16[8,48,512]{2,1,0:T(8,128)(2,1)S(1)}, u32[]{:S(2)}, u32[]{:S(2)}) async-start(bf16[8,48,512]{2,1,0:T(8,128)(2,1)} %bitcast.102), calls=%async_computation | async-start | bytes 786432 | tf_op jit(solution)/shard_map/while/body/eval_jaxpr/all_to_all | solution.py:49
  134.4 3.5 %copy-start = (f32[512,512]{0,1:T(8,128)S(1)}, f32[512,512]{0,1:T(8,128)}, u32[]{:S(2)}) copy-start(f32[512,512]{0,1:T(8,128)} %get-tuple-element.614) | copy-start | bytes 3145732 | tf_op jit(solution)/shard_map/while
  136.6 14.5 %collective-permute-start = (bf16[512,512]{1,0:T(8,128)(2,1)}, bf16[512,512]{1,0:T(8,128)(2,1)S(1)}, u32[]{:S(2)}, u32[]{:S(2)}) collective-permute-start(bf16[512,512]{1,0:T(8,128)(2,1)} %get-tuple-element.591), channel_id=1, source_target_pairs={{8,0},{16,8},{24,16},{9,1},{17,9},{25,17},{10,2},{18,10},{26,18},{... | collective-permute-start | bytes 1572872 | tf_op jit(solution)/shard_map/while/body/eval_jaxpr/ppermute | solution.py:12
  137.9 13.2 %copy-start.3 = (bf16[1,1,512,512]{3,2,1,0:T(8,128)(2,1)S(1)}, bf16[1,1,512,512]{3,2,1,0:T(8,128)(2,1)}, u32[]{:S(2)}) copy-start(bf16[1,1,512,512]{3,2,1,0:T(8,128)(2,1)} %get-tuple-element.668) | copy-start | bytes 1572868 | tf_op jit(solution)/shard_map/while
  139.6 11.6 %copy-start.1 = (f32[512,512]{0,1:T(8,128)}, f32[512,512]{0,1:T(8,128)S(1)}, u32[]{:S(2)}) copy-start(f32[512,512]{0,1:T(8,128)S(1)} %fusion.51) | copy-start | bytes 3145732 | tf_op jit(solution)/shard_map/while
  (4 other events, 3.2 us)
Sparse Core Ops, SparseCore 0:
  153.8 35.7 reduce-scatter.1
where the time goes:
time: 199 us; the launch traced here: 198 us
  waiting for transfers between devices  111 us (56%)
  other arithmetic  27.5 us (14%)
  starting transfers between devices  21.2 us (11%)
  matrix products  14.3 us (7%)
  between operations  14.1 us (7%)
  local copies, waits for them, and re-layouts  9.32 us (5%)
    ppermute x4, waiting for transfers between devices, from_behind(): return lax.ppermute(block, axis, route)  46.2 us
    reduce_scatter x1, waiting for transfers between devices, per_device(): lax.psum_scatter(final_state[2], 'dom', scatter_dimension=0, tiled=True)  35.9 us
    all_to_all x4, waiting for transfers between devices, boundary_sum(): lax.all_to_all(mirror, 'dom', split_axis=0, concat_axis=0, tiled=True)  28.9 us
    all_to_all x4, starting transfers between devices, boundary_sum(): lax.all_to_all(mirror, 'dom', split_axis=0, concat_axis=0, tiled=True)  16.1 us
    scatter-add x4, other arithmetic, boundary_sum(): jnp.zeros((row_count, feat_width), jnp.float32).at[target_index]  13.1 us
    select_n x4, other arithmetic, run_tick(): grads_out = jnp.where(active, updated, grads_out)  7.63 us
    dot_general x4, matrix products, run_tick(): jnp.einsum('ia,ib->ab', agg_block, masked, preferred_element_type=jnp.flo...  6.49 us
    ppermute x4, starting transfers between devices, from_behind(): return lax.ppermute(block, axis, route)  5.12 us
  transfers between devices with their start and end apart: 9, of which 9 were waited for; matrix products, arithmetic and copies ran while one was open for 5% of the time, Pallas kernels for 0%

commit v1 on v0

v1 whole, which is shorter than its diff:
```python
import functools
import math

import jax
import jax.numpy as jnp
from jax import lax
from jax.experimental import pallas as pl
from jax.experimental.pallas import tpu as pltpu
from jax.sharding import PartitionSpec as P

MESH = pl.DeviceIdType.MESH


def dot(a, b, dims=((1,), (0,))):
    return lax.dot_general(a, b, (dims, ((), ())), preferred_element_type=jnp.float32)


def kernel(
    sections, parts, chunk, scale,
    top, agg, pre, weight, adj, tiles, tile_source, target,
    out_grad, out_dw,
    gbuf, pbuf, wbuf, abuf, xbuf, tbuf, tfull, sbuf, zbuf, yacc, ybuf, lbuf, msend, mrecv,
    dwsend, dwown, dwrecv,
    load_sem, first_sem, zin_sem, zout_sem, feed_out, feed_in, msend_sem, mrecv_sem,
    dwsend_sem, dwrecv_sem,
):
    rows, feat = abuf.shape[0], zbuf.shape[1]
    chunks = feat // chunk
    slots = msend.shape[2] // parts
    tile_count, tile = tbuf.shape[0], tbuf.shape[1]
    shard = feat // parts
    sec = lax.axis_index("section")
    me = lax.axis_index("dom")
    top_sec = sections - 1
    is_top = sec == top_sec
    double = (lax.rem(sec, 2) == 0) & (sec < sections - 2)
    feeder = (lax.rem(sec, 2) == 1) & (sec < top_sec)
    passer = (sec > 0) & jnp.logical_not(feeder)
    begin = jnp.where(double, 0, 1)

    below = jnp.maximum(sec - 1, 0)
    below_slot = jnp.where((lax.rem(below, 2) == 0) & (below < sections - 2), 0, 1)

    loads = [
        pltpu.make_async_copy(weight.at[0], wbuf.at[1], load_sem.at[0]),
        pltpu.make_async_copy(pre.at[0, 0], pbuf.at[1], load_sem.at[1]),
        pltpu.make_async_copy(tiles.at[0], tbuf, load_sem.at[2]),
        pltpu.make_async_copy(adj.at[0], abuf, load_sem.at[3]),
        pltpu.make_async_copy(agg.at[0, 0], xbuf, load_sem.at[4]),
    ]

    def cols(c):
        return pl.ds(c * chunk, chunk)

    @pl.when(is_top)
    def _():
        for c in range(chunks):
            pltpu.make_async_copy(top.at[0, :, cols(c)], gbuf.at[1, c], first_sem.at[c]).start()

    for load in loads:
        load.start()

    barrier = pltpu.get_barrier_semaphore()
    for i in range(1, parts):
        pl.semaphore_signal(
            barrier, inc=1, device_id={"dom": lax.rem(me + i, parts)}, device_id_type=MESH
        )

    @pl.when(sec > 0)
    def _():
        pl.semaphore_signal(barrier, inc=1, device_id={"section": sec - 1}, device_id_type=MESH)

    @pl.when(sec < top_sec)
    def _():
        pl.semaphore_signal(barrier, inc=1, device_id={"section": sec + 1}, device_id_type=MESH)

    vertical = jnp.where(sec > 0, 1, 0) + jnp.where(sec < top_sec, 1, 0)
    pl.semaphore_wait(barrier, parts - 1 + vertical)

    def feed(i):
        source, dest = ((pre.at[0, 0], pbuf.at[0]), (weight.at[0], wbuf.at[0]))[i]
        return pltpu.make_async_remote_copy(
            src_ref=source, dst_ref=dest, send_sem=feed_out.at[i], recv_sem=feed_in.at[i],
            device_id={"section": below}, device_id_type=MESH,
        )

    @pl.when(feeder)
    def _():
        for i in range(2):
            feed(i).start()

    def pass_down(source_slot, c):
        return pltpu.make_async_remote_copy(
            src_ref=gbuf.at[source_slot, c], dst_ref=gbuf.at[below_slot, c],
            send_sem=zout_sem.at[c], recv_sem=zin_sem.at[c],
            device_id={"section": below}, device_id_type=MESH,
        )

    loads[2].wait()
    for b in range(tile_count):
        block = tbuf[b].astype(jnp.float32)
        for j in range(rows // tile):
            hit = (tile_source[0, b] == j).astype(jnp.float32)
            tfull[pl.ds(b * tile, tile), pl.ds(j * tile, tile)] = (block * hit).astype(jnp.bfloat16)
    loads[0].wait()
    loads[1].wait()
    loads[3].wait()

    def boundary_copy(phase, c, i):
        peer = lax.rem(me + i, parts)
        return pltpu.make_async_remote_copy(
            src_ref=msend.at[phase, c, pl.ds(pl.multiple_of(peer * slots, 16), slots)],
            dst_ref=mrecv.at[phase, c, pl.ds(pl.multiple_of(me * slots, 16), slots)],
            send_sem=msend_sem.at[phase, c, i - 1],
            recv_sem=mrecv_sem.at[phase, c, i - 1],
            device_id={"dom": peer}, device_id_type=MESH,
        )

    def boundary_arrived(phase, c, i):
        source = lax.rem(me + parts - i, parts)
        return pltpu.make_async_remote_copy(
            src_ref=msend.at[phase, c, pl.ds(pl.multiple_of(source * slots, 16), slots)],
            dst_ref=mrecv.at[phase, c, pl.ds(pl.multiple_of(source * slots, 16), slots)],
            send_sem=msend_sem.at[phase, c, i - 1],
            recv_sem=mrecv_sem.at[phase, c, i - 1],
            device_id={"dom": source}, device_id_type=MESH,
        )

    def dw_copy(i):
        peer = lax.rem(me + i, parts)
        return pltpu.make_async_remote_copy(
            src_ref=dwsend.at[peer], dst_ref=dwrecv.at[i - 1],
            send_sem=dwsend_sem.at[i - 1], recv_sem=dwrecv_sem.at[i - 1],
            device_id={"dom": peer}, device_id_type=MESH,
        )

    spot = lax.broadcasted_iota(jnp.int32, (rows, parts * slots), 0)
    sbuf[...] = jnp.where(spot == target[...], 1.0, 0.0).astype(jnp.bfloat16)

    def run_layer(phase, carry):
        @pl.when(phase == 0)
        def _():
            for i in range(2):
                feed(i).wait_recv()

        for c in range(chunks):
            @pl.when((phase == begin) & jnp.logical_not(is_top))
            def _():
                pass_down(1, c).wait_recv()

            @pl.when(is_top)
            def _():
                pltpu.make_async_copy(
                    top.at[0, :, cols(c)], gbuf.at[1, c], first_sem.at[c]
                ).wait()

            @pl.when(feeder)
            def _():
                pass_down(1, c).start()

            gradient = gbuf[phase, c].astype(jnp.float32)
            keep = pbuf[phase, :, cols(c)].astype(jnp.float32) > 0
            masked = jnp.where(keep, gradient, 0.0).astype(jnp.bfloat16)
            zbuf[:, cols(c)] = masked
            term = dot(masked, wbuf[phase, :, cols(c)], ((1,), (1,)))
            if c == 0:
                yacc[...] = term
            elif c < chunks - 1:
                yacc[...] += term
            else:
                ybuf[...] = (yacc[...] + term).astype(jnp.bfloat16)

        for c in range(chunks):
            msend[phase, c] = dot(tfull[...], ybuf[:, cols(c)]).astype(jnp.bfloat16)
            for i in range(1, parts):
                boundary_copy(phase, c, i).start()
            own = pl.ds(pl.multiple_of(me * slots, 16), slots)
            mrecv[phase, c, own, :] = msend[phase, c, own, :]

        for c in range(chunks):
            lbuf[c] = dot(abuf[...], ybuf[:, cols(c)])

        @pl.when(phase == 1)
        def _():
            loads[4].wait()
            for d in range(parts):
                part = dot(xbuf[:, pl.ds(d * shard, shard)], zbuf[...], ((0,), (0,)))
                dwsend[d] = part.astype(jnp.bfloat16)

                @pl.when(me == d)
                def _():
                    dwown[...] = part
            for i in range(1, parts):
                dw_copy(i).start()

        for c in range(chunks):
            for i in range(1, parts):
                boundary_arrived(phase, c, i).wait_recv()
            total = (lbuf[c] + dot(sbuf[...], mrecv[phase, c])).astype(jnp.bfloat16)
            gbuf[phase + 1, c] = total

            @pl.when(phase == 1)
            def _():
                @pl.when(passer)
                def _():
                    pass_down(2, c).start()

                out_grad[0, 0, :, cols(c)] = total

        for c in range(chunks):
            for i in range(1, parts):
                boundary_copy(phase, c, i).wait_send()
        return carry

    lax.fori_loop(begin, 2, run_layer, 0)

    total = dwown[...]
    for i in range(1, parts):
        dw_copy(i).wait_recv()
        total = total + dwrecv[i - 1].astype(jnp.float32)
    out_dw[0] = total * scale

    for i in range(1, parts):
        dw_copy(i).wait_send()

    @pl.when(sec > 0)
    def _():
        for c in range(chunks):
            pass_down(1, c).wait_send()

    @pl.when(feeder)
    def _():
        for i in range(2):
            feed(i).wait_send()


def per_device(
    sections, parts,
    top_grad, agg_in, pre_act, weights, local_adj_t, tiles, tile_source, owner_rows, counts,
):
    group_count, rows, feat = top_grad.shape
    assert group_count == 1
    slots = owner_rows.shape[3]
    tile_count, tile = tiles.shape[1], tiles.shape[2]
    chunk = min(128, feat)
    chunks = feat // chunk
    shard = feat // parts
    scale = 1.0 / math.sqrt(group_count * rows * parts)
    live = jnp.arange(slots)[None, :] < counts[0, 0][:, None]
    target = jnp.where(live, owner_rows[0, 0], rows).reshape(1, -1)
    wide = parts * slots
    bf16, f32 = jnp.bfloat16, jnp.float32
    dma = pltpu.SemaphoreType.DMA
    anywhere = pl.BlockSpec(memory_space=pl.ANY)
    vmem = pl.BlockSpec(memory_space=pltpu.VMEM)
    return pl.pallas_call(
        functools.partial(kernel, sections, parts, chunk, scale),
        out_shape=(
            jax.ShapeDtypeStruct((1, 1, rows, feat), bf16),
            jax.ShapeDtypeStruct((1, shard, feat), f32),
        ),
        in_specs=[anywhere] * 6 + [pl.BlockSpec(memory_space=pltpu.SMEM), vmem],
        out_specs=(vmem, vmem),
        scratch_shapes=[
            pltpu.VMEM((3, chunks, rows, chunk), bf16),
            pltpu.VMEM((2, rows, feat), bf16),
            pltpu.VMEM((2, feat, feat), bf16),
            pltpu.VMEM((rows, rows), bf16),
            pltpu.VMEM((rows, feat), bf16),
            pltpu.VMEM((tile_count, tile, tile), bf16),
            pltpu.VMEM((tile_count * tile, rows), bf16),
            pltpu.VMEM((rows, wide), bf16),
            pltpu.VMEM((rows, feat), bf16),
            pltpu.VMEM((rows, feat), f32),
            pltpu.VMEM((rows, feat), bf16),
            pltpu.VMEM((chunks, rows, chunk), f32),
            pltpu.VMEM((2, chunks, wide, chunk), bf16),
            pltpu.VMEM((2, chunks, wide, chunk), bf16),
            pltpu.VMEM((parts, shard, feat), bf16),
            pltpu.VMEM((shard, feat), f32),
            pltpu.VMEM((parts - 1, shard, feat), bf16),
            dma((5,)), dma((chunks,)), dma((chunks,)), dma((chunks,)), dma((2,)), dma((2,)),
            dma((2, chunks, parts - 1)), dma((2, chunks, parts - 1)),
            dma((parts - 1,)), dma((parts - 1,)),
        ],
        compiler_params=pltpu.CompilerParams(
            collective_id=0, has_side_effects=True, vmem_limit_bytes=50 * 1024 * 1024
        ),
    )(top_grad, agg_in, pre_act, weights, local_adj_t, tiles, tile_source, target)


def solution(mesh):
    in_specs = (
        P(None, "dom", None),
        P("section", None, "dom", None),
        P("section", None, "dom", None),
        P("section", None, None),
        P(None, "dom", None),
        P(None, "dom", None, None),
        P(None, "dom"),
        P(None, "dom", None, None),
        P(None, "dom", None),
    )
    out_specs = (P("section", None, "dom", None), P("section", "dom", None))
    return jax.shard_map(
        functools.partial(per_device, mesh.shape["section"], mesh.shape["dom"]),
        mesh=mesh, in_specs=in_specs, out_specs=out_specs, check_vma=False,
    )
```

time: 199 us -> 77.9 us (0.39)
  waiting for transfers between devices: 111 us -> 0 us
  Pallas kernels: 0 us -> 67.3 us
  other arithmetic: 27.5 us -> 0.08 us
  starting transfers between devices: 21.2 us -> 0 us
  matrix products: 14.3 us -> 0 us
  between operations: 14.1 us -> 0.69 us
    pallas_call x0 -> x1, Pallas kernels: none -> 67.3 us  [per_device(): pl.pallas_call(functools.partial(kernel, sections, parts, chunk, scale),...]
    ppermute x4 -> x0, waiting for transfers between devices: 46.2 us -> none  [from_behind(): return lax.ppermute(block, axis, route)]
    reduce_scatter x1 -> x0, waiting for transfers between devices: 35.9 us -> none  [per_device(): lax.psum_scatter(final_state[2], 'dom', scatter_dimension=0, tiled=True)]
    all_to_all x4 -> x0, waiting for transfers between devices: 28.9 us -> none  [boundary_sum(): lax.all_to_all(mirror, 'dom', split_axis=0, concat_axis=0, tiled=True)]
    all_to_all x4 -> x0, starting transfers between devices: 16.1 us -> none  [boundary_sum(): lax.all_to_all(mirror, 'dom', split_axis=0, concat_axis=0, tiled=True)]
    dot_general x16 -> x0, matrix products: 14.3 us -> none  [the longest x4 6.49 us: run_tick(): jnp.einsum('ia,ib->ab', agg_block, masked, preferred_element_type=jnp.flo...]
    scatter-add x4 -> x0, other arithmetic: 13.1 us -> none  [boundary_sum(): jnp.zeros((row_count, feat_width), jnp.float32).at[target_index]]
    select_n x16 -> x1, other arithmetic: 12.5 us -> 0.01 us  [per_device(): target = jnp.where(live, owner_rows[0, 0], rows).reshape(1, -1)]
  transfers between devices with their start and end apart: 9 -> 0, of which waited for: 9 -> 0; matrix products, arithmetic and copies ran while one was open for 5% -> 0% of each run, Pallas kernels for 0% -> 0%
where the time goes in v1:
time: 77.9 us; the launch traced here: 77.1 us
  Pallas kernels  67.3 us (86%)
  local copies, waits for them, and re-layouts  9 us (12%)
    pallas_call x1, Pallas kernels, per_device(): pl.pallas_call(functools.partial(kernel, sections, parts, chunk, scale),...  67.3 us
    unnamed x20, local copies, waits for them, and re-layouts  8.83 us

profile of v1, /device:TPU:0, one launch (start us, length us, event | category | flops | bytes accessed | tf_op | source)
XLA Modules:
  0.0 77.1 jit_solution(14514134934266009436)
XLA Ops:
  0.6 0.0 copy-start.8
  0.6 0.0 copy-start.7
  0.6 0.6 copy-done.8
  1.3 0.1 iota_compare_fusion
  1.4 0.1 lt.29
  1.5 0.0 copy-done.7
  1.5 0.1 squeeze.3
  1.5 0.0 copy-start.6
  1.6 0.6 copy-done.6
  2.2 0.0 copy-start
  2.2 1.0 %copy-done = bf16[1,512,512]{2,1,0:T(8,128)(2,1)S(1)} copy-done((bf16[1,512,512]{2,1,0:T(8,128)(2,1)S(1)}, bf16[1,512,512]{2,1,0:T(8,128)(2,1)}, u32[]{:S(2)}) %copy-start) | copy-done | bytes 524312
  3.2 0.0 copy-start.1
  3.2 1.0 %copy-done.1 = bf16[1,1,512,512]{3,2,1,0:T(8,128)(2,1)S(1)} copy-done((bf16[1,1,512,512]{3,2,1,0:T(8,128)(2,1)S(1)}, bf16[1,1,512,512]{3,2,1,0:T(8,128)(2,1)}, u32[]{:S(2)}) %copy-start.1) | copy-done | bytes 524312
  4.3 0.0 copy-start.2
  4.3 1.0 %copy-done.2 = bf16[1,1,512,512]{3,2,1,0:T(8,128)(2,1)S(1)} copy-done((bf16[1,1,512,512]{3,2,1,0:T(8,128)(2,1)S(1)}, bf16[1,1,512,512]{3,2,1,0:T(8,128)(2,1)}, u32[]{:S(2)}) %copy-start.2) | copy-done | bytes 524312
  5.3 0.0 copy-start.3
  5.3 1.0 %copy-done.3 = bf16[1,512,512]{2,1,0:T(8,128)(2,1)S(1)} copy-done((bf16[1,512,512]{2,1,0:T(8,128)(2,1)S(1)}, bf16[1,512,512]{2,1,0:T(8,128)(2,1)}, u32[]{:S(2)}) %copy-start.3) | copy-done | bytes 524312
  6.4 0.0 copy-start.4
  6.4 1.0 %copy-done.4 = bf16[1,512,512]{2,1,0:T(8,128)(2,1)S(1)} copy-done((bf16[1,512,512]{2,1,0:T(8,128)(2,1)S(1)}, bf16[1,512,512]{2,1,0:T(8,128)(2,1)}, u32[]{:S(2)}) %copy-start.4) | copy-done | bytes 524312
  7.4 0.0 copy-start.5
  7.4 0.9 %copy-done.5 = bf16[1,3,128,128]{3,2,1,0:T(8,128)(2,1)S(1)} copy-done((bf16[1,3,128,128]{3,2,1,0:T(8,128)(2,1)S(1)}, bf16[1,3,128,128]{3,2,1,0:T(8,128)(2,1)}, u32[]{:S(2)}) %copy-start.5) | copy-done | bytes 98328
  8.3 67.3 %shard_map.104 = (bf16[1,1,512,512]{3,2,1,0:T(8,128)(2,1)S(1)}, f32[1,64,512]{2,1,0:T(8,128)S(1)}) custom-call(bf16[1,512,512]{2,1,0:T(8,128)(2,1)S(1)} %copy-done, bf16[1,1,512,512]{3,2,1,0:T(8,128)(2,1)S(1)} %copy-done.1, bf16[1,1,512,512]{3,2,1,0:T(8,128)(2,1)S(1)} %copy-done.2, bf16[1,512,512]{2,1,0:T(8,128)(2,1)S(1)} %copy-done.3, ...), custom_call_target="tpu_custom_call" | custom-call | tf_op jit(solution)/shard_map/pallas_call | solution.py:256
  75.7 0.8 %copy.13 = bf16[1,1,512,512]{3,2,1,0:T(8,128)(2,1)} copy(bf16[1,1,512,512]{3,2,1,0:T(8,128)(2,1)S(1)} %get-tuple-element.4) | data formatting | bytes 1048576
  76.5 0.7 copy.14
  (1 shorter events, 0.0 us)
Async XLA Ops:
  0.6 0.7 copy-start.8
  0.6 0.8 %copy-start.7 = (s32[1,1,8,48]{3,2,1,0:T(8,128)S(1)}, s32[1,1,8,48]{3,2,1,0:T(8,128)}, u32[]{:S(2)}) copy-start(s32[1,1,8,48]{3,2,1,0:T(8,128)} %param.16) | copy-start | bytes 4612
  1.5 0.7 copy-start.6
  2.2 1.0 %copy-start = (bf16[1,512,512]{2,1,0:T(8,128)(2,1)S(1)}, bf16[1,512,512]{2,1,0:T(8,128)(2,1)}, u32[]{:S(2)}) copy-start(bf16[1,512,512]{2,1,0:T(8,128)(2,1)} %top.1) | copy-start | bytes 1572868
  3.2 1.0 %copy-start.1 = (bf16[1,1,512,512]{3,2,1,0:T(8,128)(2,1)S(1)}, bf16[1,1,512,512]{3,2,1,0:T(8,128)(2,1)}, u32[]{:S(2)}) copy-start(bf16[1,1,512,512]{3,2,1,0:T(8,128)(2,1)} %agg.1) | copy-start | bytes 1572868
  4.3 1.0 %copy-start.2 = (bf16[1,1,512,512]{3,2,1,0:T(8,128)(2,1)S(1)}, bf16[1,1,512,512]{3,2,1,0:T(8,128)(2,1)}, u32[]{:S(2)}) copy-start(bf16[1,1,512,512]{3,2,1,0:T(8,128)(2,1)} %pre.1) | copy-start | bytes 1572868
  5.3 1.0 %copy-start.3 = (bf16[1,512,512]{2,1,0:T(8,128)(2,1)S(1)}, bf16[1,512,512]{2,1,0:T(8,128)(2,1)}, u32[]{:S(2)}) copy-start(bf16[1,512,512]{2,1,0:T(8,128)(2,1)} %weight.1) | copy-start | bytes 1572868
  6.4 1.0 %copy-start.4 = (bf16[1,512,512]{2,1,0:T(8,128)(2,1)S(1)}, bf16[1,512,512]{2,1,0:T(8,128)(2,1)}, u32[]{:S(2)}) copy-start(bf16[1,512,512]{2,1,0:T(8,128)(2,1)} %adj.1) | copy-start | bytes 1572868
  7.4 0.9 %copy-start.5 = (bf16[1,3,128,128]{3,2,1,0:T(8,128)(2,1)S(1)}, bf16[1,3,128,128]{3,2,1,0:T(8,128)(2,1)}, u32[]{:S(2)}) copy-start(bf16[1,3,128,128]{3,2,1,0:T(8,128)(2,1)} %tiles.1) | copy-start | bytes 294916

commit v2 on v1

--- a/solution.py
+++ b/solution.py
@@ -17,12 +17,12 @@
 
 def kernel(
     sections, parts, chunk, scale,
-    top, agg, pre, weight, adj, tiles, tile_source, target,
+    top, agg, pre, weight, adj, tiles, tile_source, owner_rows, counts,
     out_grad, out_dw,
     gbuf, pbuf, wbuf, abuf, xbuf, tbuf, tfull, sbuf, zbuf, yacc, ybuf, lbuf, msend, mrecv,
-    dwsend, dwown, dwrecv,
+    dwfull, pairsend, pairrecv, chipsend, chiprecv, dwres,
     load_sem, first_sem, zin_sem, zout_sem, feed_out, feed_in, msend_sem, mrecv_sem,
-    dwsend_sem, dwrecv_sem,
+    pair_out, pair_in, chip_out, chip_in, out_sem, dwout_sem,
 ):
     rows, feat = abuf.shape[0], zbuf.shape[1]
     chunks = feat // chunk
@@ -126,50 +126,94 @@
             device_id={"dom": source}, device_id_type=MESH,
         )
 
-    def dw_copy(i):
-        peer = lax.rem(me + i, parts)
-        return pltpu.make_async_remote_copy(
-            src_ref=dwsend.at[peer], dst_ref=dwrecv.at[i - 1],
-            send_sem=dwsend_sem.at[i - 1], recv_sem=dwrecv_sem.at[i - 1],
+    core = lax.rem(me, 2)
+    partner = me + 1 - 2 * core
+    here = (me - core) // 2
+    chips = parts // 2
+
+    def shard_at(index):
+        return pl.ds(pl.multiple_of(index * shard, shard), shard)
+
+    def pair_copy():
+        return pltpu.make_async_remote_copy(
+            src_ref=pairsend, dst_ref=pairrecv, send_sem=pair_out, recv_sem=pair_in,
+            device_id={"dom": partner}, device_id_type=MESH,
+        )
+
+    def chip_copy(i):
+        peer = 2 * lax.rem(here + i, chips) + core
+        return pltpu.make_async_remote_copy(
+            src_ref=chipsend.at[i - 1], dst_ref=chiprecv.at[i - 1],
+            send_sem=chip_out.at[i - 1], recv_sem=chip_in.at[i - 1],
             device_id={"dom": peer}, device_id_type=MESH,
         )
 
+    def weight_terms():
+        dwfull[...] = dot(xbuf[...], zbuf[...], ((0,), (0,)))
+        for j in range(chips):
+            pairsend[j] = dwfull[shard_at(2 * j + 1 - core), :].astype(jnp.bfloat16)
+        pair_copy().start()
+
+    def weight_sums():
+        pair_copy().wait_recv()
+        for i in range(1, chips):
+            j = lax.rem(here + i, chips)
+            both = dwfull[shard_at(2 * j + core), :] + pairrecv[j].astype(jnp.float32)
+            chipsend[i - 1] = both.astype(jnp.bfloat16)
+            chip_copy(i).start()
+        dwres[...] = dwfull[shard_at(me), :] + pairrecv[here].astype(jnp.float32)
+
     spot = lax.broadcasted_iota(jnp.int32, (rows, parts * slots), 0)
-    sbuf[...] = jnp.where(spot == target[...], 1.0, 0.0).astype(jnp.bfloat16)
+    slot = lax.broadcasted_iota(jnp.int32, (1, slots), 1)
+    target = jnp.concatenate(
+        [
+            jnp.where(slot < counts[0, 0, d], owner_rows[0, 0, pl.ds(d, 1), :], rows)
+            for d in range(parts)
+        ],
+        axis=1,
+    )
+    sbuf[...] = jnp.where(spot == target, 1.0, 0.0).astype(jnp.bfloat16)
+
+    def front(phase, c, gradient):
+        keep = pbuf[phase, :, cols(c)].astype(jnp.float32) > 0
+        masked = jnp.where(keep, gradient.astype(jnp.float32), 0.0).astype(jnp.bfloat16)
+        zbuf[:, cols(c)] = masked
+        term = dot(masked, wbuf[phase, :, cols(c)], ((1,), (1,)))
+        if c == 0:
+            yacc[...] = term
+        elif c < chunks - 1:
+            yacc[...] += term
+        else:
+            ybuf[...] = (yacc[...] + term).astype(jnp.bfloat16)
+
+    def out_copy(c):
+        return pltpu.make_async_copy(
+            gbuf.at[2, c], out_grad.at[0, 0, :, cols(c)], out_sem.at[c]
+        )
+
+    @pl.when(double)
+    def _():
+        for i in range(2):
+            feed(i).wait_recv()
+
+    for c in range(chunks):
+        @pl.when(jnp.logical_not(is_top))
+        def _():
+            pass_down(1, c).wait_recv()
+
+        @pl.when(is_top)
+        def _():
+            pltpu.make_async_copy(
+                top.at[0, :, cols(c)], gbuf.at[1, c], first_sem.at[c]
+            ).wait()
+
+        @pl.when(feeder)
+        def _():
+            pass_down(1, c).start()
+
+        front(begin, c, gbuf[begin, c])
 
     def run_layer(phase, carry):
-        @pl.when(phase == 0)
-        def _():
-            for i in range(2):
-                feed(i).wait_recv()
-
-        for c in range(chunks):
-            @pl.when((phase == begin) & jnp.logical_not(is_top))
-            def _():
-                pass_down(1, c).wait_recv()
-
-            @pl.when(is_top)
-            def _():
-                pltpu.make_async_copy(
-                    top.at[0, :, cols(c)], gbuf.at[1, c], first_sem.at[c]
-                ).wait()
-
-            @pl.when(feeder)
-            def _():
-                pass_down(1, c).start()
-
-            gradient = gbuf[phase, c].astype(jnp.float32)
-            keep = pbuf[phase, :, cols(c)].astype(jnp.float32) > 0
-            masked = jnp.where(keep, gradient, 0.0).astype(jnp.bfloat16)
-            zbuf[:, cols(c)] = masked
-            term = dot(masked, wbuf[phase, :, cols(c)], ((1,), (1,)))
-            if c == 0:
-                yacc[...] = term
-            elif c < chunks - 1:
-                yacc[...] += term
-            else:
-                ybuf[...] = (yacc[...] + term).astype(jnp.bfloat16)
-
         for c in range(chunks):
             msend[phase, c] = dot(tfull[...], ybuf[:, cols(c)]).astype(jnp.bfloat16)
             for i in range(1, parts):
@@ -177,21 +221,19 @@
             own = pl.ds(pl.multiple_of(me * slots, 16), slots)
             mrecv[phase, c, own, :] = msend[phase, c, own, :]
 
+        last = phase == 1
+
+        @pl.when(last & jnp.logical_not(passer))
+        def _():
+            loads[4].wait()
+            weight_terms()
+
         for c in range(chunks):
             lbuf[c] = dot(abuf[...], ybuf[:, cols(c)])
 
-        @pl.when(phase == 1)
-        def _():
-            loads[4].wait()
-            for d in range(parts):
-                part = dot(xbuf[:, pl.ds(d * shard, shard)], zbuf[...], ((0,), (0,)))
-                dwsend[d] = part.astype(jnp.bfloat16)
-
-                @pl.when(me == d)
-                def _():
-                    dwown[...] = part
-            for i in range(1, parts):
-                dw_copy(i).start()
+        @pl.when(last & jnp.logical_not(passer))
+        def _():
+            weight_sums()
 
         for c in range(chunks):
             for i in range(1, parts):
@@ -199,39 +241,63 @@
             total = (lbuf[c] + dot(sbuf[...], mrecv[phase, c])).astype(jnp.bfloat16)
             gbuf[phase + 1, c] = total
 
-            @pl.when(phase == 1)
+            @pl.when(last)
             def _():
                 @pl.when(passer)
                 def _():
                     pass_down(2, c).start()
 
-                out_grad[0, 0, :, cols(c)] = total
-
+                out_copy(c).start()
+
+            @pl.when(jnp.logical_not(last))
+            def _():
+                front(1, c, total)
+
+        return carry
+
+    lax.fori_loop(begin, 2, run_layer, 0)
+
+    @pl.when(passer)
+    def _():
+        loads[4].wait()
+        weight_terms()
+        weight_sums()
+
+    total = dwres[...]
+    for i in range(1, chips):
+        chip_copy(i).wait_recv()
+        total = total + chiprecv[i - 1].astype(jnp.float32)
+    dwres[...] = total * scale
+    dwout = pltpu.make_async_copy(dwres, out_dw.at[0], dwout_sem)
+    dwout.start()
+
+    pair_copy().wait_send()
+    for i in range(1, chips):
+        chip_copy(i).wait_send()
+
+    @pl.when(sec > 0)
+    def _():
+        for c in range(chunks):
+            pass_down(1, c).wait_send()
+
+    @pl.when(feeder)
+    def _():
+        for i in range(2):
+            feed(i).wait_send()
+
+    def drain(phase):
         for c in range(chunks):
             for i in range(1, parts):
                 boundary_copy(phase, c, i).wait_send()
-        return carry
-
-    lax.fori_loop(begin, 2, run_layer, 0)
-
-    total = dwown[...]
-    for i in range(1, parts):
-        dw_copy(i).wait_recv()
-        total = total + dwrecv[i - 1].astype(jnp.float32)
-    out_dw[0] = total * scale
-
-    for i in range(1, parts):
-        dw_copy(i).wait_send()
-
-    @pl.when(sec > 0)
-    def _():
-        for c in range(chunks):
-            pass_down(1, c).wait_send()
-
-    @pl.when(feeder)
-    def _():
-        for i in range(2):
-            feed(i).wait_send()
+
+    @pl.when(double)
+    def _():
+        drain(0)
+
+    drain(1)
+    for c in range(chunks):
+        out_copy(c).wait()
+    dwout.wait()
 
 
 def per_device(
@@ -246,21 +312,20 @@
     chunks = feat // chunk
     shard = feat // parts
     scale = 1.0 / math.sqrt(group_count * rows * parts)
-    live = jnp.arange(slots)[None, :] < counts[0, 0][:, None]
-    target = jnp.where(live, owner_rows[0, 0], rows).reshape(1, -1)
     wide = parts * slots
     bf16, f32 = jnp.bfloat16, jnp.float32
     dma = pltpu.SemaphoreType.DMA
     anywhere = pl.BlockSpec(memory_space=pl.ANY)
     vmem = pl.BlockSpec(memory_space=pltpu.VMEM)
+    smem = pl.BlockSpec(memory_space=pltpu.SMEM)
     return pl.pallas_call(
         functools.partial(kernel, sections, parts, chunk, scale),
         out_shape=(
             jax.ShapeDtypeStruct((1, 1, rows, feat), bf16),
             jax.ShapeDtypeStruct((1, shard, feat), f32),
         ),
-        in_specs=[anywhere] * 6 + [pl.BlockSpec(memory_space=pltpu.SMEM), vmem],
-        out_specs=(vmem, vmem),
+        in_specs=[anywhere] * 6 + [smem, vmem, smem],
+        out_specs=(anywhere, anywhere),
         scratch_shapes=[
             pltpu.VMEM((3, chunks, rows, chunk), bf16),
             pltpu.VMEM((2, rows, feat), bf16),
@@ -276,17 +341,22 @@
             pltpu.VMEM((chunks, rows, chunk), f32),
             pltpu.VMEM((2, chunks, wide, chunk), bf16),
             pltpu.VMEM((2, chunks, wide, chunk), bf16),
-            pltpu.VMEM((parts, shard, feat), bf16),
+            pltpu.VMEM((feat, feat), f32),
+            pltpu.VMEM((parts // 2, shard, feat), bf16),
+            pltpu.VMEM((parts // 2, shard, feat), bf16),
+            pltpu.VMEM((parts // 2 - 1, shard, feat), bf16),
+            pltpu.VMEM((parts // 2 - 1, shard, feat), bf16),
             pltpu.VMEM((shard, feat), f32),
-            pltpu.VMEM((parts - 1, shard, feat), bf16),
             dma((5,)), dma((chunks,)), dma((chunks,)), dma((chunks,)), dma((2,)), dma((2,)),
             dma((2, chunks, parts - 1)), dma((2, chunks, parts - 1)),
-            dma((parts - 1,)), dma((parts - 1,)),
+            dma, dma, dma((parts // 2 - 1,)), dma((parts // 2 - 1,)), dma((chunks,)), dma,
         ],
         compiler_params=pltpu.CompilerParams(
-            collective_id=0, has_side_effects=True, vmem_limit_bytes=50 * 1024 * 1024
+            collective_id=0, has_side_effects=True, vmem_limit_bytes=60 * 1024 * 1024
         ),
-    )(top_grad, agg_in, pre_act, weights, local_adj_t, tiles, tile_source, target)
+    )(
+        top_grad, agg_in, pre_act, weights, local_adj_t, tiles, tile_source, owner_rows, counts
+    )
 
 
 def solution(mesh):

time: 77.9 us -> 69.4 us (0.89)
  local copies, waits for them, and re-layouts: 9 us -> 2.56 us
  Pallas kernels: 67.3 us -> 66 us
    unnamed x20 -> x4, local copies, waits for them, and re-layouts: 8.83 us -> 2.56 us
    pallas_call x1, Pallas kernels: 67.3 us -> 66 us  [per_device(): pl.pallas_call(functools.partial(kernel, sections, parts, chunk, scale),...]
where the time goes in v2:
time: 69.4 us; the launch traced here: 69.2 us
  Pallas kernels  66 us (95%)
  local copies, waits for them, and re-layouts  2.56 us (4%)
    pallas_call x1, Pallas kernels, per_device(): pl.pallas_call(functools.partial(kernel, sections, parts, chunk, scale),...  66 us
    unnamed x4, local copies, waits for them, and re-layouts  2.56 us

profile of v2, /device:TPU:0, one launch (start us, length us, event | category | flops | bytes accessed | tf_op | source)
XLA Modules:
  0.0 69.2 jit_solution(7223567978133826293)
XLA Ops:
  0.6 66.0 %shard_map.104 = (bf16[1,1,512,512]{3,2,1,0:T(8,128)(2,1)}, f32[1,64,512]{2,1,0:T(8,128)}) custom-call(bf16[1,512,512]{2,1,0:T(8,128)(2,1)} %top.1, bf16[1,1,512,512]{3,2,1,0:T(8,128)(2,1)} %agg.1, bf16[1,1,512,512]{3,2,1,0:T(8,128)(2,1)} %pre.1, bf16[1,512,512]{2,1,0:T(8,128)(2,1)} %weight.1, bf16[1,512,512]{2,1,0:T(8,128)(2,1)} %adj.1, ...), custom_call_target="tpu_custom_call" | custom-call | tf_op jit(solution)/shard_map/pallas_call | solution.py:321
  66.6 0.0 copy-start
  66.7 1.9 %copy.13 = bf16[1,1,512,512]{3,2,1,0:T(8,128)(2,1)} copy(bf16[1,1,512,512]{3,2,1,0:T(8,128)(2,1)} %get-tuple-element.4) | data formatting | bytes 1048576
  68.6 0.0 copy-done
  68.6 0.7 copy.14
Async XLA Ops:
  66.6 1.9 %copy-start = (f32[1,64,512]{2,1,0:T(8,128)S(1)}, f32[1,64,512]{2,1,0:T(8,128)}, u32[]{:S(2)}) copy-start(f32[1,64,512]{2,1,0:T(8,128)} %get-tuple-element.5) | copy-start | bytes 393220

commit v3 on v2

--- a/solution.py
+++ b/solution.py
@@ -16,7 +16,7 @@
 
 
 def kernel(
-    sections, parts, chunk, scale,
+    sections, parts, chunk, pieces, scale,
     top, agg, pre, weight, adj, tiles, tile_source, owner_rows, counts,
     out_grad, out_dw,
     gbuf, pbuf, wbuf, abuf, xbuf, tbuf, tfull, sbuf, zbuf, yacc, ybuf, lbuf, msend, mrecv,
@@ -52,14 +52,6 @@
     def cols(c):
         return pl.ds(c * chunk, chunk)
 
-    @pl.when(is_top)
-    def _():
-        for c in range(chunks):
-            pltpu.make_async_copy(top.at[0, :, cols(c)], gbuf.at[1, c], first_sem.at[c]).start()
-
-    for load in loads:
-        load.start()
-
     barrier = pltpu.get_barrier_semaphore()
     for i in range(1, parts):
         pl.semaphore_signal(
@@ -74,8 +66,13 @@
     def _():
         pl.semaphore_signal(barrier, inc=1, device_id={"section": sec + 1}, device_id_type=MESH)
 
-    vertical = jnp.where(sec > 0, 1, 0) + jnp.where(sec < top_sec, 1, 0)
-    pl.semaphore_wait(barrier, parts - 1 + vertical)
+    @pl.when(is_top)
+    def _():
+        for c in range(chunks):
+            pltpu.make_async_copy(top.at[0, :, cols(c)], gbuf.at[1, c], first_sem.at[c]).start()
+
+    for load in loads:
+        load.start()
 
     def feed(i):
         source, dest = ((pre.at[0, 0], pbuf.at[0]), (weight.at[0], wbuf.at[0]))[i]
@@ -84,15 +81,11 @@
             device_id={"section": below}, device_id_type=MESH,
         )
 
-    @pl.when(feeder)
-    def _():
-        for i in range(2):
-            feed(i).start()
-
-    def pass_down(source_slot, c):
-        return pltpu.make_async_remote_copy(
-            src_ref=gbuf.at[source_slot, c], dst_ref=gbuf.at[below_slot, c],
-            send_sem=zout_sem.at[c], recv_sem=zin_sem.at[c],
+    def pass_down(source_slot, c, r):
+        piece = pl.ds(r * (rows // pieces), rows // pieces)
+        return pltpu.make_async_remote_copy(
+            src_ref=gbuf.at[source_slot, c, piece], dst_ref=gbuf.at[below_slot, c, piece],
+            send_sem=zout_sem.at[c, r], recv_sem=zin_sem.at[c, r],
             device_id={"section": below}, device_id_type=MESH,
         )
 
@@ -102,67 +95,6 @@
         for j in range(rows // tile):
             hit = (tile_source[0, b] == j).astype(jnp.float32)
             tfull[pl.ds(b * tile, tile), pl.ds(j * tile, tile)] = (block * hit).astype(jnp.bfloat16)
-    loads[0].wait()
-    loads[1].wait()
-    loads[3].wait()
-
-    def boundary_copy(phase, c, i):
-        peer = lax.rem(me + i, parts)
-        return pltpu.make_async_remote_copy(
-            src_ref=msend.at[phase, c, pl.ds(pl.multiple_of(peer * slots, 16), slots)],
-            dst_ref=mrecv.at[phase, c, pl.ds(pl.multiple_of(me * slots, 16), slots)],
-            send_sem=msend_sem.at[phase, c, i - 1],
-            recv_sem=mrecv_sem.at[phase, c, i - 1],
-            device_id={"dom": peer}, device_id_type=MESH,
-        )
-
-    def boundary_arrived(phase, c, i):
-        source = lax.rem(me + parts - i, parts)
-        return pltpu.make_async_remote_copy(
-            src_ref=msend.at[phase, c, pl.ds(pl.multiple_of(source * slots, 16), slots)],
-            dst_ref=mrecv.at[phase, c, pl.ds(pl.multiple_of(source * slots, 16), slots)],
-            send_sem=msend_sem.at[phase, c, i - 1],
-            recv_sem=mrecv_sem.at[phase, c, i - 1],
-            device_id={"dom": source}, device_id_type=MESH,
-        )
-
-    core = lax.rem(me, 2)
-    partner = me + 1 - 2 * core
-    here = (me - core) // 2
-    chips = parts // 2
-
-    def shard_at(index):
-        return pl.ds(pl.multiple_of(index * shard, shard), shard)
-
-    def pair_copy():
-        return pltpu.make_async_remote_copy(
-            src_ref=pairsend, dst_ref=pairrecv, send_sem=pair_out, recv_sem=pair_in,
-            device_id={"dom": partner}, device_id_type=MESH,
-        )
-
-    def chip_copy(i):
-        peer = 2 * lax.rem(here + i, chips) + core
-        return pltpu.make_async_remote_copy(
-            src_ref=chipsend.at[i - 1], dst_ref=chiprecv.at[i - 1],
-            send_sem=chip_out.at[i - 1], recv_sem=chip_in.at[i - 1],
-            device_id={"dom": peer}, device_id_type=MESH,
-        )
-
-    def weight_terms():
-        dwfull[...] = dot(xbuf[...], zbuf[...], ((0,), (0,)))
-        for j in range(chips):
-            pairsend[j] = dwfull[shard_at(2 * j + 1 - core), :].astype(jnp.bfloat16)
-        pair_copy().start()
-
-    def weight_sums():
-        pair_copy().wait_recv()
-        for i in range(1, chips):
-            j = lax.rem(here + i, chips)
-            both = dwfull[shard_at(2 * j + core), :] + pairrecv[j].astype(jnp.float32)
-            chipsend[i - 1] = both.astype(jnp.bfloat16)
-            chip_copy(i).start()
-        dwres[...] = dwfull[shard_at(me), :] + pairrecv[here].astype(jnp.float32)
-
     spot = lax.broadcasted_iota(jnp.int32, (rows, parts * slots), 0)
     slot = lax.broadcasted_iota(jnp.int32, (1, slots), 1)
     target = jnp.concatenate(
@@ -173,6 +105,75 @@
         axis=1,
     )
     sbuf[...] = jnp.where(spot == target, 1.0, 0.0).astype(jnp.bfloat16)
+
+    vertical = jnp.where(sec > 0, 1, 0) + jnp.where(sec < top_sec, 1, 0)
+    pl.semaphore_wait(barrier, parts - 1 + vertical)
+
+    @pl.when(feeder)
+    def _():
+        for i in range(2):
+            feed(i).start()
+
+    loads[0].wait()
+    loads[1].wait()
+    loads[3].wait()
+
+    def boundary_copy(phase, c, i):
+        peer = lax.rem(me + i, parts)
+        return pltpu.make_async_remote_copy(
+            src_ref=msend.at[phase, c, pl.ds(pl.multiple_of(peer * slots, 16), slots)],
+            dst_ref=mrecv.at[phase, c, pl.ds(pl.multiple_of(me * slots, 16), slots)],
+            send_sem=msend_sem.at[phase, c, i - 1],
+            recv_sem=mrecv_sem.at[phase, c, i - 1],
+            device_id={"dom": peer}, device_id_type=MESH,
+        )
+
+    def boundary_arrived(phase, c, i):
+        source = lax.rem(me + parts - i, parts)
+        return pltpu.make_async_remote_copy(
+            src_ref=msend.at[phase, c, pl.ds(pl.multiple_of(source * slots, 16), slots)],
+            dst_ref=mrecv.at[phase, c, pl.ds(pl.multiple_of(source * slots, 16), slots)],
+            send_sem=msend_sem.at[phase, c, i - 1],
+            recv_sem=mrecv_sem.at[phase, c, i - 1],
+            device_id={"dom": source}, device_id_type=MESH,
+        )
+
+    core = lax.rem(me, 2)
+    partner = me + 1 - 2 * core
+    here = (me - core) // 2
+    chips = parts // 2
+
+    def shard_at(index):
+        return pl.ds(pl.multiple_of(index * shard, shard), shard)
+
+    def pair_copy():
+        return pltpu.make_async_remote_copy(
+            src_ref=pairsend, dst_ref=pairrecv, send_sem=pair_out, recv_sem=pair_in,
+            device_id={"dom": partner}, device_id_type=MESH,
+        )
+
+    def chip_copy(i):
+        peer = 2 * lax.rem(here + i, chips) + core
+        return pltpu.make_async_remote_copy(
+            src_ref=chipsend.at[i - 1], dst_ref=chiprecv.at[i - 1],
+            send_sem=chip_out.at[i - 1], recv_sem=chip_in.at[i - 1],
+            device_id={"dom": peer}, device_id_type=MESH,
+        )
+
+    def weight_terms():
+        dwfull[...] = dot(xbuf[...], zbuf[...], ((0,), (0,)))
+        for j in range(chips):
+            pairsend[j] = dwfull[shard_at(2 * j + 1 - core), :].astype(jnp.bfloat16)
+        pair_copy().start()
+
+    def weight_sums():
+        pair_copy().wait_recv()
+        for i in range(1, chips):
+            j = lax.rem(here + i, chips)
+            both = dwfull[shard_at(2 * j + core), :] + pairrecv[j].astype(jnp.float32)
+            chipsend[i - 1] = both.astype(jnp.bfloat16)
+            chip_copy(i).start()
+        dwres[...] = dwfull[shard_at(me), :] + pairrecv[here].astype(jnp.float32)
 
     def front(phase, c, gradient):
         keep = pbuf[phase, :, cols(c)].astype(jnp.float32) > 0
@@ -197,9 +198,14 @@
             feed(i).wait_recv()
 
     for c in range(chunks):
-        @pl.when(jnp.logical_not(is_top))
-        def _():
-            pass_down(1, c).wait_recv()
+        for r in range(pieces):
+            @pl.when(jnp.logical_not(is_top))
+            def _():
+                pass_down(1, c, r).wait_recv()
+
+            @pl.when(feeder)
+            def _():
+                pass_down(1, c, r).start()
 
         @pl.when(is_top)
         def _():
@@ -207,10 +213,6 @@
                 top.at[0, :, cols(c)], gbuf.at[1, c], first_sem.at[c]
             ).wait()
 
-        @pl.when(feeder)
-        def _():
-            pass_down(1, c).start()
-
         front(begin, c, gbuf[begin, c])
 
     def run_layer(phase, carry):
@@ -245,7 +247,8 @@
             def _():
                 @pl.when(passer)
                 def _():
-                    pass_down(2, c).start()
+                    for r in range(pieces):
+                        pass_down(2, c, r).start()
 
                 out_copy(c).start()
 
@@ -278,7 +281,8 @@
     @pl.when(sec > 0)
     def _():
         for c in range(chunks):
-            pass_down(1, c).wait_send()
+            for r in range(pieces):
+                pass_down(1, c, r).wait_send()
 
     @pl.when(feeder)
     def _():
@@ -310,6 +314,7 @@
     tile_count, tile = tiles.shape[1], tiles.shape[2]
     chunk = min(128, feat)
     chunks = feat // chunk
+    pieces = 4
     shard = feat // parts
     scale = 1.0 / math.sqrt(group_count * rows * parts)
     wide = parts * slots
@@ -319,7 +324,7 @@
     vmem = pl.BlockSpec(memory_space=pltpu.VMEM)
     smem = pl.BlockSpec(memory_space=pltpu.SMEM)
     return pl.pallas_call(
-        functools.partial(kernel, sections, parts, chunk, scale),
+        functools.partial(kernel, sections, parts, chunk, pieces, scale),
         out_shape=(
             jax.ShapeDtypeStruct((1, 1, rows, feat), bf16),
             jax.ShapeDtypeStruct((1, shard, feat), f32),
@@ -347,7 +352,7 @@
             pltpu.VMEM((parts // 2 - 1, shard, feat), bf16),
             pltpu.VMEM((parts // 2 - 1, shard, feat), bf16),
             pltpu.VMEM((shard, feat), f32),
-            dma((5,)), dma((chunks,)), dma((chunks,)), dma((chunks,)), dma((2,)), dma((2,)),
+            dma((5,)), dma((chunks,)), dma((chunks, pieces)), dma((chunks, pieces)), dma((2,)), dma((2,)),
             dma((2, chunks, parts - 1)), dma((2, chunks, parts - 1)),
             dma, dma, dma((parts // 2 - 1,)), dma((parts // 2 - 1,)), dma((chunks,)), dma,
         ],

time: 69.4 us -> 67.9 us (0.978)
  Pallas kernels: 66 us -> 64.5 us
    pallas_call x1, Pallas kernels: 66 us -> 64.5 us  [per_device(): pl.pallas_call(functools.partial(kernel, sections, parts, chunk, pieces,...]
where the time goes in v3:
time: 67.9 us; the launch traced here: 67.7 us
  Pallas kernels  64.5 us (95%)
  local copies, waits for them, and re-layouts  2.56 us (4%)
    pallas_call x1, Pallas kernels, per_device(): pl.pallas_call(functools.partial(kernel, sections, parts, chunk, pieces,...  64.5 us
    unnamed x4, local copies, waits for them, and re-layouts  2.56 us

profile of v3, /device:TPU:0, one launch (start us, length us, event | category | flops | bytes accessed | tf_op | source)
XLA Modules:
  0.0 67.7 jit_solution(16436590167845852871)
XLA Ops:
  0.6 64.5 %shard_map.104 = (bf16[1,1,512,512]{3,2,1,0:T(8,128)(2,1)}, f32[1,64,512]{2,1,0:T(8,128)}) custom-call(bf16[1,512,512]{2,1,0:T(8,128)(2,1)} %top.1, bf16[1,1,512,512]{3,2,1,0:T(8,128)(2,1)} %agg.1, bf16[1,1,512,512]{3,2,1,0:T(8,128)(2,1)} %pre.1, bf16[1,512,512]{2,1,0:T(8,128)(2,1)} %weight.1, bf16[1,512,512]{2,1,0:T(8,128)(2,1)} %adj.1, ...), custom_call_target="tpu_custom_call" | custom-call | tf_op jit(solution)/shard_map/pallas_call | solution.py:326
  65.1 0.0 copy-start
  65.1 1.9 %copy.13 = bf16[1,1,512,512]{3,2,1,0:T(8,128)(2,1)} copy(bf16[1,1,512,512]{3,2,1,0:T(8,128)(2,1)} %get-tuple-element.4) | data formatting | bytes 1048576
  67.0 0.0 copy-done
  67.0 0.7 copy.14
Async XLA Ops:
  65.1 1.9 %copy-start = (f32[1,64,512]{2,1,0:T(8,128)S(1)}, f32[1,64,512]{2,1,0:T(8,128)}, u32[]{:S(2)}) copy-start(f32[1,64,512]{2,1,0:T(8,128)} %get-tuple-element.5) | copy-start | bytes 393220
